TPU v7x, 32 devices: a whole 2x2x4 slice. The times are simulated.
32 devices in a mesh: expert: 4 (over z), seq: 4 (over y, x), dp: 2 (over core).
Axes of the slice: x: 2, y: 2, z: 4, core: 2. Of those that a mesh axis runs over, the one named last changes fastest.
Arguments:
- grad_out: bfloat16 [8, 512, 2048], P(('expert', 'dp'), 'seq'), may hold values from -6 to 6
- expert_ids: int32 [8, 512, 2], P(('expert', 'dp'), 'seq'), may hold values from 0 to 3, all different within a row; in each aligned block of 128 rows (0 to 127, 128 to 255, ..., all dimensions but the last counted through in order) at most 112 rows name the same one
- gate_weights: float32 [8, 512, 2], P(('expert', 'dp'), 'seq'), may hold values from 0.1 to 0.9
- hidden: bfloat16 [8, 512, 2, 7168], P(('expert', 'dp'), 'seq'), may hold values from -0.3125 to 0.3125
- queries: bfloat16 [8, 512, 2048], P(('expert', 'dp'), 'seq')
- keys: bfloat16 [8, 512, 512], P(('expert', 'dp'), 'seq')
- values: bfloat16 [8, 512, 512], P(('expert', 'dp'), 'seq'), may hold values from -6 to 6
Outputs:
- expert_grad: bfloat16 [4, 7168, 2048], P('expert', ('seq', 'dp'))
- grad_queries: bfloat16 [8, 512, 2048], P(('expert', 'dp'), 'seq')
- grad_keys: bfloat16 [8, 512, 512], P(('expert', 'dp'), 'seq')
- grad_values: bfloat16 [8, 512, 512], P(('expert', 'dp'), 'seq')
Inputs may be any that keep to these rules, and one draw needn't show every extreme that they name: `expert_ids`: each position names two different experts; among the 128 positions of one device no expert is named more than 112 times.
All inputs are finite; a program needn't handle non-finite values.
Results may differ from a plain program's by a relative error of at most 0.018.
Values may be sent and summed in bfloat16 or wider, within the bound.
A program may use at most 128 MiB of HBM per device.

v0:
```python
import jax
import jax.numpy as jnp
from jax import lax
from jax.sharding import PartitionSpec as P

HEADS = 16
KV_HEADS = 4
HEAD_DIM = 128


def expert_grads(grad_out, expert_ids, gate_weights, hidden):
    experts = lax.axis_size("expert")
    shards = lax.axis_size("seq")
    pair_size = lax.axis_size("dp")
    tokens = grad_out.shape[1]
    model_width = grad_out.shape[2]
    unit_piece = hidden.shape[3] // shards
    owner_piece = unit_piece // pair_size
    row_count = tokens * 2
    capacity = 7 * tokens // (2 * experts)
    flat_ids = expert_ids.reshape(row_count)
    scaled = (gate_weights[0][..., None] * grad_out[0][:, None, :].astype(jnp.float32)).astype(
        jnp.bfloat16
    )
    scaled = scaled.reshape(row_count, model_width)
    onehot = (flat_ids[:, None] == jnp.arange(experts, dtype=jnp.int32)[None, :]).astype(jnp.int32)
    before = jnp.cumsum(onehot, axis=0) - onehot
    slot_index = jnp.sum(before * onehot, axis=1)
    flat_hidden = hidden.reshape(row_count, shards, unit_piece)
    hidden_send = jnp.zeros((experts, shards, capacity, unit_piece), jnp.bfloat16)
    hidden_send = hidden_send.at[flat_ids, :, slot_index, :].set(flat_hidden)
    spread = jnp.broadcast_to(scaled[:, None, :], (row_count, shards, model_width))
    grad_send = jnp.zeros((experts, shards, capacity, model_width), jnp.bfloat16)
    grad_send = grad_send.at[flat_ids, :, slot_index, :].set(spread)
    grad_recv, hidden_recv = (
        lax.all_to_all(
            grad_send.reshape(experts * shards, capacity, model_width),
            ("expert", "seq"),
            split_axis=0,
            concat_axis=0,
            tiled=True,
        ),
        lax.all_to_all(
            hidden_send.reshape(experts * shards, capacity, unit_piece),
            ("expert", "seq"),
            split_axis=0,
            concat_axis=0,
            tiled=True,
        ),
    )
    grad_rows = grad_recv.reshape(-1, model_width)
    hidden_rows = hidden_recv.reshape(-1, unit_piece)
    local_grad = lax.psum_scatter(
        lax.dot_general(
            hidden_rows, grad_rows, (((0,), (0,)), ((), ())), preferred_element_type=jnp.float32
        ).astype(jnp.bfloat16),
        "dp",
        scatter_dimension=0,
        tiled=True,
    )
    return local_grad.reshape(1, owner_piece, model_width)


def attention_grads(queries, keys, values, grad_out):
    per_group = HEADS // KV_HEADS
    score_scale = HEAD_DIM ** (-0.5)
    tokens = queries.shape[1]
    whole_keys, whole_values = (
        lax.all_gather(keys, "seq", axis=1, tiled=True),
        lax.all_gather(values, "seq", axis=1, tiled=True),
    )
    key_count = whole_keys.shape[1]
    query_heads = queries[0].reshape(tokens, KV_HEADS, per_group, HEAD_DIM)
    out_heads = grad_out[0].reshape(tokens, KV_HEADS, per_group, HEAD_DIM)
    key_heads = whole_keys[0].reshape(key_count, KV_HEADS, HEAD_DIM)
    value_heads = whole_values[0].reshape(key_count, KV_HEADS, HEAD_DIM)
    scores = (
        jnp.einsum("qhgd,khd->hgqk", query_heads, key_heads, preferred_element_type=jnp.float32)
        * score_scale
    )
    row_max = jnp.max(scores, axis=-1, keepdims=True)
    raised = jnp.exp(scores - row_max)
    probabilities = raised / jnp.sum(raised, axis=-1, keepdims=True)
    probs_low = probabilities.astype(jnp.bfloat16)
    dprobs = jnp.einsum(
        "qhgd,khd->hgqk", out_heads, value_heads, preferred_element_type=jnp.float32
    )
    row_delta = jnp.sum(probabilities * dprobs, axis=-1, keepdims=True)
    dscores = (probabilities * (dprobs - row_delta)).astype(jnp.bfloat16)
    value_part = jnp.einsum(
        "hgqk,qhgd->khd", probs_low, out_heads, preferred_element_type=jnp.float32
    )
    key_part = (
        jnp.einsum("hgqk,qhgd->khd", dscores, query_heads, preferred_element_type=jnp.float32)
        * score_scale
    )
    grad_q = (
        jnp.einsum("hgqk,khd->qhgd", dscores, key_heads, preferred_element_type=jnp.float32)
        * score_scale
    )
    key_sums, value_sums = (
        lax.psum_scatter(
            key_part.reshape(1, key_count, KV_HEADS * HEAD_DIM).astype(jnp.bfloat16),
            "seq",
            scatter_dimension=1,
            tiled=True,
        ).astype(jnp.float32),
        lax.psum_scatter(
            value_part.reshape(1, key_count, KV_HEADS * HEAD_DIM).astype(jnp.bfloat16),
            "seq",
            scatter_dimension=1,
            tiled=True,
        ).astype(jnp.float32),
    )
    grad_queries = grad_q.reshape(1, tokens, HEADS * HEAD_DIM).astype(jnp.bfloat16)
    return (grad_queries, key_sums.astype(jnp.bfloat16), value_sums.astype(jnp.bfloat16))


def on_device(grad_out, expert_ids, gate_weights, hidden, queries, keys, values):
    expert_grad = expert_grads(grad_out, expert_ids, gate_weights, hidden)
    grad_queries, grad_keys, grad_values = attention_grads(queries, keys, values, grad_out)
    return (expert_grad, grad_queries, grad_keys, grad_values)


def solution(mesh):
    in_specs = (
        P(("expert", "dp"), "seq", None),
        P(("expert", "dp"), "seq", None),
        P(("expert", "dp"), "seq", None),
        P(("expert", "dp"), "seq", None, None),
        P(("expert", "dp"), "seq", None),
        P(("expert", "dp"), "seq", None),
        P(("expert", "dp"), "seq", None),
    )
    out_specs = (
        P("expert", ("seq", "dp"), None),
        P(("expert", "dp"), "seq", None),
        P(("expert", "dp"), "seq", None),
        P(("expert", "dp"), "seq", None),
    )
    return jax.shard_map(
        on_device, mesh=mesh, in_specs=in_specs, out_specs=out_specs, check_vma=False
    )
```

profile of v0, /device:TPU:0, one launch (start us, length us, event | category | flops | bytes accessed | tf_op | source)
XLA Modules:
  0.0 443.8 jit_solution(10077372838262434562)
XLA Ops:
  10.0 9.8 %reshape.163 = bf16[256,4,1792]{2,1,0:T(4,128)(2,1)} reshape(bf16[1,128,2,7168]{3,2,1,0:T(2,128)(2,1)} %param.10) | data formatting | bytes 7340032 | tf_op jit(solution)/shard_map/reshape | solution.py:29
  19.8 4.3 broadcast_in_dim.6
  24.2 36.0 %scatter_fusion = bf16[4,4,112,1792]{3,1,2,0:T(4,128)(2,1)} fusion(bf16[4,4,112,1792]{3,1,2,0:T(4,128)(2,1)} %broadcast_in_dim.6, s32[256]{0:T(256)S(1)} %bitcast.98, bf16[256,4,1792]{2,1,0:T(4,128)(2,1)} %reshape.163), kind=kCustom, calls=%fused_computation | custom fusion | bytes 11012096 | tf_op jit(solution)/shard_map/scatter | solution.py:31
  60.2 6.3 %copy.31 = bf16[4,4,112,1792]{3,2,1,0:T(8,128)(2,1)} copy(bf16[4,4,112,1792]{3,1,2,0:T(4,128)(2,1)} %scatter_fusion) | data formatting | bytes 12845056 | tf_op jit(solution)/shard_map/scatter | solution.py:31
  66.5 8.5 %all-to-all-start = ((bf16[16,112,1792]{2,1,0:T(8,128)(2,1)}), bf16[16,112,1792]{2,1,0:T(8,128)(2,1)}, u32[]{:S(2)}, u32[]{:S(2)}) async-start(bf16[16,112,1792]{2,1,0:T(8,128)(2,1)} %bitcast.101), calls=%async_computation | async-start | bytes 12845056 | tf_op jit(solution)/shard_map/all_to_all | solution.py:43
  75.2 2.5 mul.56
  77.7 2.7 mul.57
  80.8 4.2 broadcast_in_dim.8
  85.1 6.7 %broadcast_in_dim.7 = bf16[4,4,112,2048]{3,1,2,0:T(4,128)(2,1)} broadcast(bf16[]{:T(256)} %constant.7.clone.1), dimensions={} | broadcast | bytes 7340034 | tf_op jit(solution)/shard_map/broadcast_in_dim | solution.py:33
  91.8 36.4 %scatter_fusion.1 = bf16[4,4,112,2048]{3,1,2,0:T(4,128)(2,1)} fusion(bf16[4,4,112,2048]{3,1,2,0:T(4,128)(2,1)} %broadcast_in_dim.7, s32[256]{0:T(256)S(1)} %bitcast.99, bf16[256,4,2048]{2,1,0:T(4,128)(2,1)} %broadcast_in_dim.8), kind=kCustom, calls=%fused_computation.1 | custom fusion | bytes 12584960 | tf_op jit(solution)/shard_map/scatter | solution.py:34
  128.1 10.2 %copy.33 = bf16[4,4,112,2048]{3,2,1,0:T(8,128)(2,1)} copy(bf16[4,4,112,2048]{3,1,2,0:T(4,128)(2,1)} %scatter_fusion.1) | data formatting | bytes 14680064 | tf_op jit(solution)/shard_map/scatter | solution.py:34
  138.3 57.2 %all-to-all-done = bf16[16,112,1792]{2,1,0:T(8,128)(2,1)} async-done(((bf16[16,112,1792]{2,1,0:T(8,128)(2,1)}), bf16[16,112,1792]{2,1,0:T(8,128)(2,1)}, u32[]{:S(2)}, u32[]{:S(2)}) %all-to-all-start) | async-done | bytes 6422560 | tf_op jit(solution)/shard_map/all_to_all | solution.py:43
  195.5 30.8 %all-to-all-start.1 = ((bf16[16,112,2048]{2,1,0:T(8,128)(2,1)}), bf16[16,112,2048]{2,1,0:T(8,128)(2,1)}, u32[]{:S(2)}, u32[]{:S(2)}) async-start(bf16[16,112,2048]{2,1,0:T(8,128)(2,1)} %bitcast.100), calls=%async_computation.1 | async-start | bytes 14680064 | tf_op jit(solution)/shard_map/all_to_all | solution.py:36
  227.2 48.6 %all_gather.6 = bf16[1,512,512]{1,2,0:T(8,128)(2,1)S(1)} all-gather(bf16[1,128,512]{1,2,0:T(8,128)(2,1)S(1)} %copy.34), channel_id=1, replica_groups=mesh['expert'=4,'seq'=4,'dp'=2] {'seq'}, dimensions={1}, use_global_device_ids=true | all-gather | bytes 655360 | tf_op jit(solution)/shard_map/all_gather | solution.py:69
  275.8 18.1 %all_gather.7 = bf16[1,512,512]{1,2,0:T(8,128)(2,1)S(1)} all-gather(bf16[1,128,512]{1,2,0:T(8,128)(2,1)S(1)} %copy.37), channel_id=1, replica_groups=mesh['expert'=4,'seq'=4,'dp'=2] {'seq'}, dimensions={1}, use_global_device_ids=true | all-gather | bytes 655360 | tf_op jit(solution)/shard_map/all_gather | solution.py:70
  293.9 3.4 fusion.28
  297.4 3.1 fusion.1
  303.5 2.1 copy.43
  305.6 3.8 fusion.18
  309.5 2.1 copy.46
  311.6 49.2 %all-to-all-done.1 = bf16[16,112,2048]{2,1,0:T(8,128)(2,1)} async-done(((bf16[16,112,2048]{2,1,0:T(8,128)(2,1)}), bf16[16,112,2048]{2,1,0:T(8,128)(2,1)}, u32[]{:S(2)}, u32[]{:S(2)}) %all-to-all-start.1) | async-done | bytes 7340064 | tf_op jit(solution)/shard_map/all_to_all | solution.py:36
  360.8 19.6 %bitcast_convert_fusion = bf16[1792,2048]{1,0:T(8,128)(2,1)} fusion(bf16[16,112,1792]{2,1,0:T(8,128)(2,1)} %all-to-all-done, bf16[16,112,2048]{2,1,0:T(8,128)(2,1)} %all-to-all-done.1), kind=kOutput, calls=%fused_computation.3 | convolution fusion | flops 13157007360 | bytes 21102592 | tf_op jit(solution)/shard_map/dot_general | solution.py:54
  382.0 36.6 %reduce-scatter.8.cloned.1.call-done = bf16[1,128,512]{2,1,0:T(8,128)(2,1)} async-done(((bf16[1,512,512]{2,1,0:T(8,128)(2,1)}), bf16[1,128,512]{2,1,0:T(8,128)(2,1)}) %reduce-scatter.8.cloned.1.call-update) | async-done | bytes 131088 | tf_op jit(solution)/shard_map/reduce_scatter | solution.py:108
  418.5 18.7 %reduce-scatter.4.cloned.1.call-done = bf16[896,2048]{1,0:T(8,128)(2,1)} async-done(((bf16[1792,2048]{1,0:T(8,128)(2,1)}), bf16[896,2048]{1,0:T(8,128)(2,1)}) %reduce-scatter.4.cloned.1.call-update) | async-done | bytes 3670032 | tf_op jit(solution)/shard_map/reduce_scatter | solution.py:53
  (49 shorter events, 8.8 us)
Async XLA Ops:
  66.5 8.5 %copy-start.1 = (bf16[1,128,2048]{2,1,0:T(8,128)(2,1)S(1)}, bf16[1,128,2048]{2,1,0:T(8,128)(2,1)}, u32[]{:S(2)}) copy-start(bf16[1,128,2048]{2,1,0:T(8,128)(2,1)} %param.7) | copy-start | bytes 1572868
  66.5 129.0 %all-to-all-start = ((bf16[16,112,1792]{2,1,0:T(8,128)(2,1)}), bf16[16,112,1792]{2,1,0:T(8,128)(2,1)}, u32[]{:S(2)}, u32[]{:S(2)}) async-start(bf16[16,112,1792]{2,1,0:T(8,128)(2,1)} %bitcast.101), calls=%async_computation | async-start | bytes 12845056 | tf_op jit(solution)/shard_map/all_to_all | solution.py:43
  75.0 5.3 %copy-start.7 = (f32[1,128,2]{1,2,0:T(2,128)S(1)}, f32[1,128,2]{1,2,0:T(2,128)}, u32[]{:S(2)}) copy-start(f32[1,128,2]{1,2,0:T(2,128)} %param.9) | copy-start | bytes 3076
  195.5 31.1 %copy-start.5 = (bf16[1,128,512]{2,1,0:T(8,128)(2,1)S(1)}, bf16[1,128,512]{2,1,0:T(8,128)(2,1)}, u32[]{:S(2)}) copy-start(bf16[1,128,512]{2,1,0:T(8,128)(2,1)} %param.12) | copy-start | bytes 393220
  195.5 31.2 %copy-start.2 = (bf16[1,128,2048]{2,1,0:T(8,128)(2,1)S(1)}, bf16[1,128,2048]{2,1,0:T(8,128)(2,1)}, u32[]{:S(2)}) copy-start(bf16[1,128,2048]{2,1,0:T(8,128)(2,1)} %param.11) | copy-start | bytes 1572868
  195.5 31.5 %copy-start.6 = (bf16[1,128,512]{2,1,0:T(8,128)(2,1)S(1)}, bf16[1,128,512]{2,1,0:T(8,128)(2,1)}, u32[]{:S(2)}) copy-start(bf16[1,128,512]{2,1,0:T(8,128)(2,1)} %param.13) | copy-start | bytes 393220
  195.5 165.3 %all-to-all-start.1 = ((bf16[16,112,2048]{2,1,0:T(8,128)(2,1)}), bf16[16,112,2048]{2,1,0:T(8,128)(2,1)}, u32[]{:S(2)}, u32[]{:S(2)}) async-start(bf16[16,112,2048]{2,1,0:T(8,128)(2,1)} %bitcast.100), calls=%async_computation.1 | async-start | bytes 14680064 | tf_op jit(solution)/shard_map/all_to_all | solution.py:36
  226.3 155.7 %reduce-scatter.6.cloned.1.call-start = ((), (), s32[]{:S(2)}) async-start(), calls=%async_computation.6 | async-start | bytes 655360 | tf_op jit(solution)/shard_map/reduce_scatter | solution.py:102
  227.0 73.5 %copy-start.3 = (bf16[1,128,2048]{1,2,0:T(8,128)(2,1)}, bf16[1,128,2048]{1,2,0:T(8,128)(2,1)S(1)}, u32[]{:S(2)}) copy-start(bf16[1,128,2048]{1,2,0:T(8,128)(2,1)S(1)} %copy.60) | copy-start | bytes 1572868
  297.4 3.4 copy-start
  300.8 1.0 copy-start.4
  305.6 112.9 %reduce-scatter.8.cloned.1.call-start = ((), (), s32[]{:S(2)}) async-start(), calls=%async_computation.7 | async-start | bytes 655360 | tf_op jit(solution)/shard_map/reduce_scatter | solution.py:108
  311.5 125.7 %reduce-scatter.4.cloned.1.call-start = ((), (), s32[]{:S(2)}) async-start(), calls=%async_computation.5 | async-start | bytes 11010048 | tf_op jit(solution)/shard_map/reduce_scatter | solution.py:53
Sparse Core Ops, SparseCore 0:
  305.7 72.4 reduce-scatter.5
  381.8 36.6 reduce-scatter.7
  421.4 15.8 reduce-scatter.3
where the time goes:
time: 445 us; the launch traced here: 444 us
  waiting for transfers between devices  162 us (36%)
  local copies, waits for them, and re-layouts  127 us (29%)
  blocking collectives  66.8 us (15%)
  starting transfers between devices  39.4 us (9%)
  matrix products  32.1 us (7%)
  between operations  13.9 us (3%)
    all_to_all x1, waiting for transfers between devices, expert_grads(): lax.all_to_all(hidden_send.reshape(experts * shards, capacity, unit_piece...  57.2 us
    all_to_all x1, waiting for transfers between devices, expert_grads(): lax.all_to_all(grad_send.reshape(experts * shards, capacity, model_width)...  49.2 us
    all_gather x1, blocking collectives, attention_grads(): lax.all_gather(keys, 'seq', axis=1, tiled=True)  48.6 us
    scatter x2, local copies, waits for them, and re-layouts, expert_grads(): grad_send = grad_send.at[flat_ids, :, slot_index, :].set(spread)  46.5 us
    scatter x2, local copies, waits for them, and re-layouts, expert_grads(): hidden_send = hidden_send.at[flat_ids, :, slot_index, :].set(flat_hidden)  42.3 us
    reduce_scatter x1, waiting for transfers between devices, attention_grads(): lax.psum_scatter(value_part.reshape(1, key_count, KV_HEADS * HEAD_DIM).as...  36.6 us
    all_to_all x1, starting transfers between devices, expert_grads(): lax.all_to_all(grad_send.reshape(experts * shards, capacity, model_width)...  30.8 us
    dot_general x1, matrix products, expert_grads(): lax.dot_general(hidden_rows, grad_rows, (((0,), (0,)), ((), ())), preferr...  19.6 us
  transfers between devices with their start and end apart: 5, of which 4 were waited for; matrix products, arithmetic and copies ran while one was open for 23% of the time, Pallas kernels for 0%

commit v1 on v0

--- a/solution.py
+++ b/solution.py
@@ -6,6 +6,28 @@
 HEADS = 16
 KV_HEADS = 4
 HEAD_DIM = 128
+
+
+def split_up(value, dim, length):
+    before, after = (value.shape[:dim], value.shape[dim + 1 :])
+    return jnp.moveaxis(value.reshape(*before, length, -1, *after), dim, 0)
+
+
+def in_order(pieces, dim):
+    lengths = list(pieces.shape[1:])
+    lengths[dim] *= pieces.shape[0]
+    return jnp.moveaxis(pieces, 0, dim).reshape(lengths)
+
+
+def pairwise_exchange(value, axis, split_dim, concat_dim):
+    count, index = (lax.axis_size(axis), lax.axis_index(axis))
+    tiles = split_up(value, split_dim, count)
+    outs = [tiles[index]]
+    for step in range(1, count):
+        sent = tiles[index ^ step]
+        outs.append(lax.ppermute(sent, axis, [(i, i ^ step) for i in range(count)]))
+    tiles = jnp.stack(outs)[index ^ jnp.arange(count)]
+    return in_order(tiles, concat_dim)
 
 
 def expert_grads(grad_out, expert_ids, gate_weights, hidden):
@@ -40,12 +62,8 @@
             concat_axis=0,
             tiled=True,
         ),
-        lax.all_to_all(
-            hidden_send.reshape(experts * shards, capacity, unit_piece),
-            ("expert", "seq"),
-            split_axis=0,
-            concat_axis=0,
-            tiled=True,
+        pairwise_exchange(
+            hidden_send.reshape(experts * shards, capacity, unit_piece), ("expert", "seq"), 0, 0
         ),
     )
     grad_rows = grad_recv.reshape(-1, model_width)

time: 445 us -> 489 us (1.099)
  starting transfers between devices: 39.4 us -> 76.8 us
  local copies, waits for them, and re-layouts: 127 us -> 155 us
  waiting for transfers between devices: 162 us -> 137 us
    ppermute x0 -> x15, waiting for transfers between devices: none -> 77.4 us  [pairwise_exchange(): outs.append(lax.ppermute(sent, axis, [(i, i ^ step) for i in range(count)]))]
    ppermute x0 -> x15, starting transfers between devices: none -> 68 us  [pairwise_exchange(): outs.append(lax.ppermute(sent, axis, [(i, i ^ step) for i in range(count)]))]
    all_to_all x1 -> x0, waiting for transfers between devices: 57.2 us -> none  [expert_grads(): lax.all_to_all(hidden_send.reshape(experts * shards, capacity, unit_piece...]
    all_to_all x1, waiting for transfers between devices: 49.2 us -> 0.01 us  [expert_grads(): lax.all_to_all(grad_send.reshape(experts * shards, capacity, model_width)...]
    reduce_scatter x1, waiting for transfers between devices: 18.7 us -> 59.8 us  [expert_grads(): lax.psum_scatter(lax.dot_general(hidden_rows, grad_rows, (((0,), (0,)), (...]
    reduce_scatter x1, waiting for transfers between devices: 36.6 us -> 0.01 us  [attention_grads(): lax.psum_scatter(value_part.reshape(1, key_count, KV_HEADS * HEAD_DIM).as...]
    all_to_all x1, starting transfers between devices: 30.8 us -> 8.48 us  [expert_grads(): lax.all_to_all(grad_send.reshape(experts * shards, capacity, model_width)...]
    unnamed x21 -> x41, local copies, waits for them, and re-layouts: 2.77 us -> 17.6 us
  transfers between devices with their start and end apart: 5 -> 19, of which waited for: 4 -> 9; matrix products, arithmetic and copies ran while one was open for 23% -> 25% of each run, Pallas kernels for 0% -> 0%
where the time goes in v1:
time: 489 us; the launch traced here: 488 us
  local copies, waits for them, and re-layouts  155 us (32%)
  waiting for transfers between devices  137 us (28%)
  starting transfers between devices  76.8 us (16%)
  blocking collectives  71 us (15%)
  matrix products  30 us (6%)
  between operations  14.1 us (3%)
    ppermute x15, waiting for transfers between devices, pairwise_exchange(): outs.append(lax.ppermute(sent, axis, [(i, i ^ step) for i in range(count)]))  77.4 us
    ppermute x15, starting transfers between devices, pairwise_exchange(): outs.append(lax.ppermute(sent, axis, [(i, i ^ step) for i in range(count)]))  68 us
    reduce_scatter x1, waiting for transfers between devices, expert_grads(): lax.psum_scatter(lax.dot_general(hidden_rows, grad_rows, (((0,), (0,)), (...  59.8 us
    all_gather x1, blocking collectives, attention_grads(): lax.all_gather(keys, 'seq', axis=1, tiled=True)  49.9 us
    scatter x2, local copies, waits for them, and re-layouts, expert_grads(): grad_send = grad_send.at[flat_ids, :, slot_index, :].set(spread)  46.5 us
    scatter x2, local copies, waits for them, and re-layouts, expert_grads(): hidden_send = hidden_send.at[flat_ids, :, slot_index, :].set(flat_hidden)  42.4 us
    all_gather x1, blocking collectives, attention_grads(): lax.all_gather(values, 'seq', axis=1, tiled=True)  21.2 us
    dot_general x1, matrix products, expert_grads(): lax.dot_general(hidden_rows, grad_rows, (((0,), (0,)), ((), ())), preferr...  19.6 us
  transfers between devices with their start and end apart: 19, of which 9 were waited for; matrix products, arithmetic and copies ran while one was open for 25% of the time, Pallas kernels for 0%

profile of v1, /device:TPU:0, one launch (start us, length us, event | category | flops | bytes accessed | tf_op | source)
XLA Modules:
  0.0 487.8 jit_solution(14571326137381581391)
XLA Ops:
  21.1 6.7 %broadcast_in_dim.7 = bf16[4,4,112,2048]{3,1,2,0:T(4,128)(2,1)} broadcast(bf16[]{:T(256)} %constant.24.clone.1), dimensions={} | broadcast | bytes 7340034 | tf_op jit(solution)/shard_map/broadcast_in_dim | solution.py:55
  27.8 36.3 %scatter_fusion.1 = bf16[4,4,112,2048]{3,1,2,0:T(4,128)(2,1)} fusion(bf16[4,4,112,2048]{3,1,2,0:T(4,128)(2,1)} %broadcast_in_dim.7, s32[256]{0:T(256)S(1)} %bitcast.161, bf16[256,4,2048]{2,1,0:T(4,128)(2,1)} %broadcast_in_dim.8), kind=kCustom, calls=%fused_computation.2 | custom fusion | bytes 12584960 | tf_op jit(solution)/shard_map/scatter | solution.py:56
  64.1 10.2 %copy.31 = bf16[4,4,112,2048]{3,2,1,0:T(8,128)(2,1)} copy(bf16[4,4,112,2048]{3,1,2,0:T(4,128)(2,1)} %scatter_fusion.1) | data formatting | bytes 14680064 | tf_op jit(solution)/shard_map/scatter | solution.py:56
  74.3 8.5 %all-to-all-start = ((bf16[16,112,2048]{2,1,0:T(8,128)(2,1)}), bf16[16,112,2048]{2,1,0:T(8,128)(2,1)}, u32[]{:S(2)}, u32[]{:S(2)}) async-start(bf16[16,112,2048]{2,1,0:T(8,128)(2,1)} %bitcast.163), calls=%async_computation | async-start | bytes 14680064 | tf_op jit(solution)/shard_map/all_to_all | solution.py:58
  83.7 49.9 %all_gather.6 = bf16[1,512,512]{1,2,0:T(8,128)(2,1)S(1)} all-gather(bf16[1,128,512]{1,2,0:T(8,128)(2,1)S(1)} %copy.32), channel_id=1, replica_groups=mesh['expert'=4,'seq'=4,'dp'=2] {'seq'}, dimensions={1}, use_global_device_ids=true | all-gather | bytes 655360 | tf_op jit(solution)/shard_map/all_gather | solution.py:87
  133.6 21.2 %all_gather.7 = bf16[1,512,512]{1,2,0:T(8,128)(2,1)S(1)} all-gather(bf16[1,128,512]{1,2,0:T(8,128)(2,1)S(1)} %copy.35), channel_id=1, replica_groups=mesh['expert'=4,'seq'=4,'dp'=2] {'seq'}, dimensions={1}, use_global_device_ids=true | all-gather | bytes 655360 | tf_op jit(solution)/shard_map/all_gather | solution.py:88
  166.3 9.8 %reshape.187 = bf16[256,4,1792]{2,1,0:T(4,128)(2,1)} reshape(bf16[1,128,2,7168]{3,2,1,0:T(2,128)(2,1)} %param.10) | data formatting | bytes 7340032 | tf_op jit(solution)/shard_map/reshape | solution.py:51
  176.1 4.3 broadcast_in_dim.6
  180.4 36.0 %scatter_fusion = bf16[4,4,112,1792]{3,1,2,0:T(4,128)(2,1)} fusion(bf16[4,4,112,1792]{3,1,2,0:T(4,128)(2,1)} %broadcast_in_dim.6, s32[256]{0:T(256)S(1)} %bitcast.162, bf16[256,4,1792]{2,1,0:T(4,128)(2,1)} %reshape.187), kind=kCustom, calls=%fused_computation.1 | custom fusion | bytes 11012096 | tf_op jit(solution)/shard_map/scatter | solution.py:53
  216.4 6.4 %copy.29 = bf16[4,4,112,1792]{3,2,1,0:T(8,128)(2,1)} copy(bf16[4,4,112,1792]{3,1,2,0:T(4,128)(2,1)} %scatter_fusion) | data formatting | bytes 12845056 | tf_op jit(solution)/shard_map/scatter | solution.py:53
  222.8 5.7 %dynamic-slice_bitcast_fusion = (bf16[1,112,1792]{2,1,0:T(8,128)(2,1)}, bf16[1,112,1792]{2,1,0:T(8,128)(2,1)}, bf16[1,112,1792]{2,1,0:T(8,128)(2,1)}, bf16[1,112...) fusion(bf16[16,1,112,1792]{3,2,0,1:T(8,128)(2,1)} %bitcast.164,, ...), kind=kLoop, calls=%fused_computation.43 | loop fusion | bytes 12845120 | tf_op jit(solution)/shard_map/squeeze | solution.py:27
  228.5 26.9 %collective-permute-start = (bf16[1,112,1792]{2,1,0:T(8,128)(2,1)}, bf16[1,112,1792]{2,1,0:T(8,128)(2,1)}, u32[]{:S(2)}, u32[]{:S(2)}) collective-permute-start(bf16[1,112,1792]{2,1,0:T(8,128)(2,1)} %get-tuple-element.26), channel_id=1, source_target_pairs={{0,2},{2,0},{4,6},{6,4},{8,10},{10,8},{12,14},{14,12},{16,18},{18,... | collective-permute-start | bytes 1204232 | tf_op jit(solution)/shard_map/ppermute | solution.py:28
  275.7 8.2 %collective-permute-done.2 = bf16[1,112,1792]{2,1,0:T(8,128)(2,1)} collective-permute-done((bf16[1,112,1792]{2,1,0:T(8,128)(2,1)}, bf16[1,112,1792]{2,1,0:T(8,128)(2,1)}, u32[]{:S(2)}, u32[]{:S(2)}) %collective-permute-start.2) | collective-permute-done | bytes 401440 | tf_op jit(solution)/shard_map/ppermute | solution.py:28
  285.7 11.9 %collective-permute-start.8 = (bf16[1,112,1792]{2,1,0:T(8,128)(2,1)}, bf16[1,112,1792]{2,1,0:T(8,128)(2,1)S(1)}, u32[]{:S(2)}, u32[]{:S(2)}) collective-permute-start(bf16[1,112,1792]{2,1,0:T(8,128)(2,1)} %get-tuple-element.18), channel_id=1, source_target_pairs={{0,18},{2,16},{4,22},{6,20},{8,26},{10,24},{12,30},{14,28},{16,2},... | collective-permute-start | bytes 1204232 | tf_op jit(solution)/shard_map/ppermute | solution.py:28
  300.1 5.4 %collective-permute-done.5 = bf16[1,112,1792]{2,1,0:T(8,128)(2,1)S(1)} collective-permute-done((bf16[1,112,1792]{2,1,0:T(8,128)(2,1)}, bf16[1,112,1792]{2,1,0:T(8,128)(2,1)S(1)}, u32[]{:S(2)}, u32[]{:S(2)}) %collective-permute-start.5) | collective-permute-done | bytes 401440 | tf_op jit(solution)/shard_map/ppermute | solution.py:28
  306.3 6.3 %collective-permute-done.6 = bf16[1,112,1792]{2,1,0:T(8,128)(2,1)S(1)} collective-permute-done((bf16[1,112,1792]{2,1,0:T(8,128)(2,1)}, bf16[1,112,1792]{2,1,0:T(8,128)(2,1)S(1)}, u32[]{:S(2)}, u32[]{:S(2)}) %collective-permute-start.6) | collective-permute-done | bytes 401440 | tf_op jit(solution)/shard_map/ppermute | solution.py:28
  313.4 26.8 %collective-permute-done.7 = bf16[1,112,1792]{2,1,0:T(8,128)(2,1)S(1)} collective-permute-done((bf16[1,112,1792]{2,1,0:T(8,128)(2,1)}, bf16[1,112,1792]{2,1,0:T(8,128)(2,1)S(1)}, u32[]{:S(2)}, u32[]{:S(2)}) %collective-permute-start.7) | collective-permute-done | bytes 401440 | tf_op jit(solution)/shard_map/ppermute | solution.py:28
  340.9 15.0 %collective-permute-done.8 = bf16[1,112,1792]{2,1,0:T(8,128)(2,1)S(1)} collective-permute-done((bf16[1,112,1792]{2,1,0:T(8,128)(2,1)}, bf16[1,112,1792]{2,1,0:T(8,128)(2,1)S(1)}, u32[]{:S(2)}, u32[]{:S(2)}) %collective-permute-start.8) | collective-permute-done | bytes 401440 | tf_op jit(solution)/shard_map/ppermute | solution.py:28
  355.9 6.1 %collective-permute-start.13 = (bf16[1,112,1792]{2,1,0:T(8,128)(2,1)}, bf16[1,112,1792]{2,1,0:T(8,128)(2,1)S(1)}, u32[]{:S(2)}, u32[]{:S(2)}) collective-permute-start(bf16[1,112,1792]{2,1,0:T(8,128)(2,1)} %get-tuple-element.13), channel_id=1, source_target_pairs={{0,28},{2,30},{4,24},{6,26},{8,20},{10,22},{12,16},{14,18},{16,12}... | collective-permute-start | bytes 1204232 | tf_op jit(solution)/shard_map/ppermute | solution.py:28
  362.8 16.4 %collective-permute-start.14 = (bf16[1,112,1792]{2,1,0:T(8,128)(2,1)}, bf16[1,112,1792]{2,1,0:T(8,128)(2,1)S(1)}, u32[]{:S(2)}, u32[]{:S(2)}) collective-permute-start(bf16[1,112,1792]{2,1,0:T(8,128)(2,1)} %get-tuple-element.12), channel_id=1, source_target_pairs={{0,30},{2,28},{4,26},{6,24},{8,22},{10,20},{12,18},{14,16},{16,14}... | collective-permute-start | bytes 1204232 | tf_op jit(solution)/shard_map/ppermute | solution.py:28
  379.9 9.9 %collective-permute-done.10 = bf16[1,112,1792]{2,1,0:T(8,128)(2,1)S(1)} collective-permute-done((bf16[1,112,1792]{2,1,0:T(8,128)(2,1)}, bf16[1,112,1792]{2,1,0:T(8,128)(2,1)S(1)}, u32[]{:S(2)}, u32[]{:S(2)}) %collective-permute-start.10) | collective-permute-done | bytes 401440 | tf_op jit(solution)/shard_map/ppermute | solution.py:28
  393.8 6.5 %gather_fusion = bf16[16,112,1792]{2,1,0:T(8,128)(2,1)} fusion(bf16[16,112,1792]{2,1,0:T(8,128)(2,1)} %bitcast.165, s32[1024]{0:T(1024)S(1)} %pad_clamp_fusion), kind=kCustom, calls=%fused_computation | custom fusion | bytes 12845120 | tf_op jit(solution)/shard_map/gather | solution.py:29
  400.3 19.6 %convolution_convert_fusion = bf16[1792,2048]{1,0:T(8,128)(2,1)} fusion(bf16[1792,1792]{1,0:T(8,128)(2,1)} %bitcast.166, bf16[1792,2048]{1,0:T(8,128)(2,1)} %bitcast.40), kind=kOutput, calls=%fused_computation.4 | convolution fusion | flops 13157007360 | bytes 21102592 | tf_op jit(solution)/shard_map/dot_general | solution.py:72
  421.4 59.8 %reduce-scatter.4.cloned.1.call-done = bf16[896,2048]{1,0:T(8,128)(2,1)} async-done(((bf16[1792,2048]{1,0:T(8,128)(2,1)}), bf16[896,2048]{1,0:T(8,128)(2,1)}) %reduce-scatter.4.cloned.1.call-update) | async-done | bytes 3670032 | tf_op jit(solution)/shard_map/reduce_scatter | solution.py:71
  (102 shorter events, 60.3 us)
Async XLA Ops:
  7.2 9.2 %copy-start.10 = (f32[1,128,2]{1,2,0:T(2,128)S(1)}, f32[1,128,2]{1,2,0:T(2,128)}, u32[]{:S(2)}) copy-start(f32[1,128,2]{1,2,0:T(2,128)} %param.9) | copy-start | bytes 3076
  74.3 9.3 %copy-start.7 = (bf16[1,128,512]{2,1,0:T(8,128)(2,1)S(1)}, bf16[1,128,512]{2,1,0:T(8,128)(2,1)}, u32[]{:S(2)}) copy-start(bf16[1,128,512]{2,1,0:T(8,128)(2,1)} %param.13) | copy-start | bytes 393220
  74.3 326.0 %all-to-all-start = ((bf16[16,112,2048]{2,1,0:T(8,128)(2,1)}), bf16[16,112,2048]{2,1,0:T(8,128)(2,1)}, u32[]{:S(2)}, u32[]{:S(2)}) async-start(bf16[16,112,2048]{2,1,0:T(8,128)(2,1)} %bitcast.163), calls=%async_computation | async-start | bytes 14680064 | tf_op jit(solution)/shard_map/all_to_all | solution.py:58
  82.7 338.7 %reduce-scatter.6.cloned.1.call-start = ((), (), s32[]{:S(2)}) async-start(), calls=%async_computation.5 | async-start | bytes 655360 | tf_op jit(solution)/shard_map/reduce_scatter | solution.py:120
  83.6 77.8 %copy-start.4 = (bf16[1,128,2048]{1,2,0:T(8,128)(2,1)}, bf16[1,128,2048]{1,2,0:T(8,128)(2,1)S(1)}, u32[]{:S(2)}) copy-start(bf16[1,128,2048]{1,2,0:T(8,128)(2,1)S(1)} %copy.58) | copy-start | bytes 1572868
  166.2 255.2 %reduce-scatter.8.cloned.1.call-start = ((), (), s32[]{:S(2)}) async-start(), calls=%async_computation.6 | async-start | bytes 655360 | tf_op jit(solution)/shard_map/reduce_scatter | solution.py:126
  222.8 39.0 %copy-start.1 = (f32[4,4,128,512]{2,3,1,0:T(8,128)S(1)}, f32[4,4,128,512]{2,3,1,0:T(8,128)}, u32[]{:S(2)}) copy-start(f32[4,4,128,512]{2,3,1,0:T(8,128)} %get-tuple-element.29) | copy-start | bytes 12582916
  222.8 39.0 %copy-start.9 = (f32[4,4,128]{2,1,0:T(4,128)S(1)}, f32[4,4,128]{2,1,0:T(4,128)}, u32[]{:S(2)}) copy-start(f32[4,4,128]{2,1,0:T(4,128)} %copy-done.8) | copy-start | bytes 24580
  228.5 40.7 %collective-permute-start = (bf16[1,112,1792]{2,1,0:T(8,128)(2,1)}, bf16[1,112,1792]{2,1,0:T(8,128)(2,1)}, u32[]{:S(2)}, u32[]{:S(2)}) collective-permute-start(bf16[1,112,1792]{2,1,0:T(8,128)(2,1)} %get-tuple-element.26), channel_id=1, source_target_pairs={{0,2},{2,0},{4,6},{6,4},{8,10},{10,8},{12,14},{14,12},{16,18},{18,... | collective-permute-start | bytes 1204232 | tf_op jit(solution)/shard_map/ppermute | solution.py:28
  255.4 18.2 %collective-permute-start.1 = (bf16[1,112,1792]{2,1,0:T(8,128)(2,1)}, bf16[1,112,1792]{2,1,0:T(8,128)(2,1)}, u32[]{:S(2)}, u32[]{:S(2)}) collective-permute-start(bf16[1,112,1792]{2,1,0:T(8,128)(2,1)} %get-tuple-element.25), channel_id=1, source_target_pairs={{0,4},{2,6},{4,0},{6,2},{8,12},{10,14},{12,8},{14,10},{16,20},{18,... | collective-permute-start | bytes 1204232 | tf_op jit(solution)/shard_map/ppermute | solution.py:28
  258.4 25.4 %collective-permute-start.2 = (bf16[1,112,1792]{2,1,0:T(8,128)(2,1)}, bf16[1,112,1792]{2,1,0:T(8,128)(2,1)}, u32[]{:S(2)}, u32[]{:S(2)}) collective-permute-start(bf16[1,112,1792]{2,1,0:T(8,128)(2,1)} %get-tuple-element.24), channel_id=1, source_target_pairs={{0,6},{2,4},{4,2},{6,0},{8,14},{10,12},{12,10},{14,8},{16,22},{18,... | collective-permute-start | bytes 1204232 | tf_op jit(solution)/shard_map/ppermute | solution.py:28
  259.8 25.9 %collective-permute-start.3 = (bf16[1,112,1792]{2,1,0:T(8,128)(2,1)}, bf16[1,112,1792]{2,1,0:T(8,128)(2,1)}, u32[]{:S(2)}, u32[]{:S(2)}) collective-permute-start(bf16[1,112,1792]{2,1,0:T(8,128)(2,1)} %get-tuple-element.23), channel_id=1, source_target_pairs={{0,8},{2,10},{4,12},{6,14},{8,0},{10,2},{12,4},{14,6},{16,24},{18,... | collective-permute-start | bytes 1204232 | tf_op jit(solution)/shard_map/ppermute | solution.py:28
  259.8 39.5 %collective-permute-start.4 = (bf16[1,112,1792]{2,1,0:T(8,128)(2,1)}, bf16[1,112,1792]{2,1,0:T(8,128)(2,1)S(1)}, u32[]{:S(2)}, u32[]{:S(2)}) collective-permute-start(bf16[1,112,1792]{2,1,0:T(8,128)(2,1)} %get-tuple-element.22), channel_id=1, source_target_pairs={{0,10},{2,8},{4,14},{6,12},{8,2},{10,0},{12,6},{14,4},{16,26},{18,... | collective-permute-start | bytes 1204232 | tf_op jit(solution)/shard_map/ppermute | solution.py:28
  265.5 215.7 %reduce-scatter.4.cloned.1.call-start = ((), (), s32[]{:S(2)}) async-start(), calls=%async_computation.4 | async-start | bytes 11010048 | tf_op jit(solution)/shard_map/reduce_scatter | solution.py:71
  269.2 36.3 %collective-permute-start.5 = (bf16[1,112,1792]{2,1,0:T(8,128)(2,1)}, bf16[1,112,1792]{2,1,0:T(8,128)(2,1)S(1)}, u32[]{:S(2)}, u32[]{:S(2)}) collective-permute-start(bf16[1,112,1792]{2,1,0:T(8,128)(2,1)} %get-tuple-element.21), channel_id=1, source_target_pairs={{0,12},{2,14},{4,8},{6,10},{8,4},{10,6},{12,0},{14,2},{16,28},{18,... | collective-permute-start | bytes 1204232 | tf_op jit(solution)/shard_map/ppermute | solution.py:28
  273.6 39.0 %collective-permute-start.6 = (bf16[1,112,1792]{2,1,0:T(8,128)(2,1)}, bf16[1,112,1792]{2,1,0:T(8,128)(2,1)S(1)}, u32[]{:S(2)}, u32[]{:S(2)}) collective-permute-start(bf16[1,112,1792]{2,1,0:T(8,128)(2,1)} %get-tuple-element.20), channel_id=1, source_target_pairs={{0,14},{2,12},{4,10},{6,8},{8,6},{10,4},{12,2},{14,0},{16,30},{18,... | collective-permute-start | bytes 1204232 | tf_op jit(solution)/shard_map/ppermute | solution.py:28
  283.9 56.3 %collective-permute-start.7 = (bf16[1,112,1792]{2,1,0:T(8,128)(2,1)}, bf16[1,112,1792]{2,1,0:T(8,128)(2,1)S(1)}, u32[]{:S(2)}, u32[]{:S(2)}) collective-permute-start(bf16[1,112,1792]{2,1,0:T(8,128)(2,1)} %get-tuple-element.19), channel_id=1, source_target_pairs={{0,16},{2,18},{4,20},{6,22},{8,24},{10,26},{12,28},{14,30},{16,0},... | collective-permute-start | bytes 1204232 | tf_op jit(solution)/shard_map/ppermute | solution.py:28
  285.7 70.2 %collective-permute-start.8 = (bf16[1,112,1792]{2,1,0:T(8,128)(2,1)}, bf16[1,112,1792]{2,1,0:T(8,128)(2,1)S(1)}, u32[]{:S(2)}, u32[]{:S(2)}) collective-permute-start(bf16[1,112,1792]{2,1,0:T(8,128)(2,1)} %get-tuple-element.18), channel_id=1, source_target_pairs={{0,18},{2,16},{4,22},{6,20},{8,26},{10,24},{12,30},{14,28},{16,2},... | collective-permute-start | bytes 1204232 | tf_op jit(solution)/shard_map/ppermute | solution.py:28
  299.3 63.5 %collective-permute-start.9 = (bf16[1,112,1792]{2,1,0:T(8,128)(2,1)}, bf16[1,112,1792]{2,1,0:T(8,128)(2,1)S(1)}, u32[]{:S(2)}, u32[]{:S(2)}) collective-permute-start(bf16[1,112,1792]{2,1,0:T(8,128)(2,1)} %get-tuple-element.17), channel_id=1, source_target_pairs={{0,20},{2,22},{4,16},{6,18},{8,28},{10,30},{12,24},{14,26},{16,4},... | collective-permute-start | bytes 1204232 | tf_op jit(solution)/shard_map/ppermute | solution.py:28
  305.5 84.4 %collective-permute-start.10 = (bf16[1,112,1792]{2,1,0:T(8,128)(2,1)}, bf16[1,112,1792]{2,1,0:T(8,128)(2,1)S(1)}, u32[]{:S(2)}, u32[]{:S(2)}) collective-permute-start(bf16[1,112,1792]{2,1,0:T(8,128)(2,1)} %get-tuple-element.16), channel_id=1, source_target_pairs={{0,22},{2,20},{4,18},{6,16},{8,30},{10,28},{12,26},{14,24},{16,6},... | collective-permute-start | bytes 1204232 | tf_op jit(solution)/shard_map/ppermute | solution.py:28
  312.6 78.1 %collective-permute-start.11 = (bf16[1,112,1792]{2,1,0:T(8,128)(2,1)}, bf16[1,112,1792]{2,1,0:T(8,128)(2,1)S(1)}, u32[]{:S(2)}, u32[]{:S(2)}) collective-permute-start(bf16[1,112,1792]{2,1,0:T(8,128)(2,1)} %get-tuple-element.15), channel_id=1, source_target_pairs={{0,24},{2,26},{4,28},{6,30},{8,16},{10,18},{12,20},{14,22},{16,8},... | collective-permute-start | bytes 1204232 | tf_op jit(solution)/shard_map/ppermute | solution.py:28
  340.1 51.3 %collective-permute-start.12 = (bf16[1,112,1792]{2,1,0:T(8,128)(2,1)}, bf16[1,112,1792]{2,1,0:T(8,128)(2,1)S(1)}, u32[]{:S(2)}, u32[]{:S(2)}) collective-permute-start(bf16[1,112,1792]{2,1,0:T(8,128)(2,1)} %get-tuple-element.14), channel_id=1, source_target_pairs={{0,26},{2,24},{4,30},{6,28},{8,18},{10,16},{12,22},{14,20},{16,10}... | collective-permute-start | bytes 1204232 | tf_op jit(solution)/shard_map/ppermute | solution.py:28
  355.9 36.3 %collective-permute-start.13 = (bf16[1,112,1792]{2,1,0:T(8,128)(2,1)}, bf16[1,112,1792]{2,1,0:T(8,128)(2,1)S(1)}, u32[]{:S(2)}, u32[]{:S(2)}) collective-permute-start(bf16[1,112,1792]{2,1,0:T(8,128)(2,1)} %get-tuple-element.13), channel_id=1, source_target_pairs={{0,28},{2,30},{4,24},{6,26},{8,20},{10,22},{12,16},{14,18},{16,12}... | collective-permute-start | bytes 1204232 | tf_op jit(solution)/shard_map/ppermute | solution.py:28
  362.8 30.2 %collective-permute-start.14 = (bf16[1,112,1792]{2,1,0:T(8,128)(2,1)}, bf16[1,112,1792]{2,1,0:T(8,128)(2,1)S(1)}, u32[]{:S(2)}, u32[]{:S(2)}) collective-permute-start(bf16[1,112,1792]{2,1,0:T(8,128)(2,1)} %get-tuple-element.12), channel_id=1, source_target_pairs={{0,30},{2,28},{4,26},{6,24},{8,22},{10,20},{12,18},{14,16},{16,14}... | collective-permute-start | bytes 1204232 | tf_op jit(solution)/shard_map/ppermute | solution.py:28
  (6 other events, 34.1 us)
Sparse Core Ops, SparseCore 0:
  166.3 75.2 reduce-scatter.5
  265.7 42.6 reduce-scatter.7
  420.0 61.1 reduce-scatter.3
